TPU v7x, 32 devices: a whole 2x2x4 slice. The times are simulated.
32 devices in a mesh: grp: 2 (over y), blk: 4 (over z), sub: 2 (over x), frq: 2 (over core).
Axes of the slice: x: 2, y: 2, z: 4, core: 2. Of those that a mesh axis runs over, the one named last changes fastest.
Arguments:
- spectra: bfloat16 [2, 8192, 4096], P(None, ('grp', 'blk'), ('sub', 'frq')), parts along dimension 1, may hold values from -6 to 6
- channel_mask: int32 [8, 1024], P(('grp', 'blk')), parts along dimension 0, may hold values 0 or 1
- local_channel: int32 [8, 4, 48], P(('grp', 'blk')), parts along dimension 0, may hold values from 0 to 1023
- partner_channel: int32 [8, 4, 48], P(('grp', 'blk')), parts along dimension 0, may hold values from 0 to 31
- stack_owner: int32 [8, 4, 48, 1], P(('grp', 'blk')), parts along dimension 0, may hold values from 0 to 3; in each aligned block of 192 rows (0 to 191, 192 to 383, ..., all dimensions but the last counted through in order) at most 96 rows name the same one
- stack_slot: int32 [8, 4, 48], P(('grp', 'blk')), parts along dimension 0, may hold values from 0 to 31
Outputs:
- stacks: float32 [256, 1024], P(('grp', 'blk'), ('sub', 'frq')), parts along dimension 0
There are 2 independent parts, one for each index of `grp`. A program takes and returns all parts, laid end to end along the dimension named above; each array names one. Nothing has to cross between parts.
Inputs may be any that keep to these rules, and one draw needn't show every extreme that they name: `stack_owner`: of the pairs of one source block, at most 96 name one owner, a bound that some block reaches of them.
All inputs are finite; a program needn't handle non-finite values. No bound on the sum of `channel_mask` on one device may be relied on, other than what follows from the above.
Results may differ from a plain program's by a relative error of at most 0.009.
Values may be sent and summed in bfloat16 or wider, within the bound.
A program may use at most 64 MiB of HBM per device.

v0:
```python
import math
import jax
import jax.numpy as jnp
from jax import lax
from jax.sharding import PartitionSpec as P

NF = 4096
LAGS = 1024
VS_BLK = 32
SLOTS_DEV = 32
CAP = 96


def from_root(block, axis, owner):
    block = jnp.where(lax.axis_index(axis) == owner, block, jnp.zeros_like(block))
    return lax.psum(block, axis)


def lag_rows(first_bin, bin_count):
    bin_index = first_bin + jnp.arange(bin_count, dtype=jnp.int32)
    shifts = jnp.arange(LAGS, dtype=jnp.int32) - LAGS // 2
    phase_angle = jnp.mod(bin_index[:, None] * shifts[None, :], NF).astype(jnp.float32) * (
        2.0 * math.pi / NF
    )
    factor = 1.0 / math.sqrt(NF)
    return jnp.concatenate(
        [jnp.cos(phase_angle) * factor, -jnp.sin(phase_angle) * factor], axis=0
    ).astype(jnp.bfloat16)


def per_device(spectra, channel_mask, local_channel, partner_channel, stack_owner, stack_slot):
    blocks = lax.axis_size("blk")
    bins_here = spectra.shape[2]
    lag_table = lag_rows(lax.axis_index(("sub", "frq")) * bins_here, bins_here)
    masked = spectra * channel_mask[0].astype(jnp.bfloat16)[None, :, None]
    stride_size = masked.shape[1] // VS_BLK
    own_panel = masked.reshape(2, VS_BLK, stride_size, bins_here)[:, :, 0, :]
    local_rows = local_channel[0]
    partner_rows = partner_channel[0]
    pair_step = local_rows.shape[1]
    empty_terms = jnp.zeros((blocks * pair_step, lag_table.shape[1]), jnp.float32)

    def add_pairs(partial_terms, panel_data, source):
        own_pick = lax.dynamic_index_in_dim(local_rows, source, 0, keepdims=False)
        partner_pick = lax.dynamic_index_in_dim(partner_rows, source, 0, keepdims=False)
        own_spectra = jnp.take(masked, own_pick, axis=1).astype(jnp.float32)
        partner_spectra = jnp.take(panel_data, partner_pick, axis=1).astype(jnp.float32)
        real_part = (
            own_spectra[0] * partner_spectra[0] + own_spectra[1] * partner_spectra[1]
        ).astype(jnp.bfloat16)
        imag_part = (
            own_spectra[1] * partner_spectra[0] - own_spectra[0] * partner_spectra[1]
        ).astype(jnp.bfloat16)
        cross_rows = jnp.concatenate([real_part, imag_part], axis=1)
        products = jnp.dot(cross_rows, lag_table, preferred_element_type=jnp.float32)
        start_row = (source * pair_step).astype(jnp.int32)
        return lax.dynamic_update_slice_in_dim(partial_terms, products, start_row, 0)

    def root_turn(turn_index, partial_terms):
        panel_data = from_root(own_panel, "blk", turn_index)
        return add_pairs(partial_terms, panel_data, turn_index)

    partial_terms = lax.fori_loop(0, blocks, root_turn, empty_terms)
    summed = lax.psum_scatter(
        partial_terms.astype(jnp.bfloat16), ("sub", "frq"), scatter_dimension=1, tiled=True
    )
    owners = stack_owner[0].reshape(-1)
    slots_flat = stack_slot[0].reshape(-1)
    lag_width = summed.shape[1]
    owner_hits = (owners[:, None] == jnp.arange(blocks, dtype=jnp.int32)[None, :]).astype(jnp.int32)
    earlier_hits = jnp.cumsum(owner_hits, axis=0) - owner_hits
    bucket_rank = jnp.sum(earlier_hits * owner_hits, axis=1)
    targets = owners * CAP + bucket_rank
    outgoing = jnp.zeros((blocks * CAP, lag_width), jnp.bfloat16).at[targets].set(summed)
    labels = (
        jnp.full((blocks * CAP,), -1.0, jnp.bfloat16)
        .at[targets]
        .set(slots_flat.astype(jnp.bfloat16))
    )
    arrived, arrived_labels = (
        lax.all_to_all(
            outgoing.reshape(blocks, CAP, lag_width), "blk", split_axis=0, concat_axis=0, tiled=True
        ),
        lax.all_to_all(labels.reshape(blocks, CAP), "blk", split_axis=0, concat_axis=0, tiled=True),
    )
    slot_ids = arrived_labels.reshape(-1).astype(jnp.int32)
    selector = (jnp.arange(SLOTS_DEV, dtype=jnp.int32)[:, None] == slot_ids[None, :]).astype(
        jnp.bfloat16
    )
    result_stacks = jnp.dot(
        selector, arrived.reshape(blocks * CAP, lag_width), preferred_element_type=jnp.float32
    )
    return result_stacks


def solution(mesh):
    return jax.shard_map(
        per_device,
        mesh=mesh,
        in_specs=(
            P(None, ("grp", "blk"), ("sub", "frq")),
            P(("grp", "blk"), None),
            P(("grp", "blk"), None, None),
            P(("grp", "blk"), None, None),
            P(("grp", "blk"), None, None, None),
            P(("grp", "blk"), None, None),
        ),
        out_specs=P(("grp", "blk"), ("sub", "frq")),
        check_vma=False,
    )
```

profile of v0, /device:TPU:0, one launch (start us, length us, event | category | flops | bytes accessed | tf_op | source)
XLA Modules:
  0.0 259.1 jit_solution(5674109913671485158)
XLA Ops:
  7.4 0.7 convert_reduce_fusion
  8.1 2.5 broadcast_multiply_fusion
  10.6 6.2 %copy.30 = bf16[2,1024,1024]{2,0,1:T(2,128)(2,1)} copy(bf16[2,1024,1024]{2,1,0:T(8,128)(2,1)S(1)} %broadcast_multiply_fusion) | data formatting | bytes 8388608 | tf_op jit(solution)/shard_map/while | solution.py:63
  16.9 0.2 slice.58
  17.0 0.2 copy.42
  17.3 17.6 %multiply_convert_fusion.1 = (bf16[1024,1024]{1,0:T(8,128)(2,1)S(1)}, bf16[1024,1024]{1,0:T(8,128)(2,1)S(1)}) fusion(s32[1024]{0:T(1024)S(1)} %get-tuple-element.182, s32[1024]{0:T(1024)S(1)} %get-tuple-element.183), kind=kLoop, calls=%fused_computation.40 | loop fusion | flops 19922944 | bytes 4202496 | tf_op jit(solution)/shard_map/convert.4
  34.9 2.4 pad_maximum_fusion
  37.4 176.2 %while.13 = (s32[]{:T(128)}, bf16[192,1024]{1,0:T(8,128)(2,1)S(1)}, s32[4,48]{1,0:T(4,128)S(1)}, bf16[2,1024,1024]{2,0,1:T(2,128)(2,1)}, s32[4,48]{1,0:T(4,128)S...) while((s32[]{:T(128)}, bf16[192,1024]{1,0:T(8,128)(2,1)S(1)}, ...), condition=%wide.region_6.7_spmd, body=%wide.region_4.6_spmd.sunk | while | flops 202640240 | bytes 8989001 | solution.py:63
  37.4 0.0 all-reduce.3.cloned.1.call-start
  37.4 0.7 broadcast_select_fusion.4
  38.3 3.1 %gather_fusion.1 = bf16[48,2,1024]{2,1,0:T(2,128)(2,1)S(1)} fusion(bf16[2,1024,1024]{2,0,1:T(2,128)(2,1)} %get-tuple-element.268, s32[1024]{0:T(1024)S(1)} %pad_clamp_fusion.5), kind=kCustom, calls=%fused_computation.clone.1 | custom fusion | bytes 393408 | tf_op jit(solution)/shard_map/while/body/eval_jaxpr/jit(_take)/gather | solution.py:46
  41.4 0.2 convert_bitcast_fusion.5
  41.7 36.2 %all-reduce.3.cloned.1.call-done = bf16[2,32,1024]{2,0,1:T(2,128)(2,1)} async-done(((bf16[2,32,1024]{2,0,1:T(2,128)(2,1)}), bf16[2,32,1024]{2,0,1:T(2,128)(2,1)}) %all-reduce.3.cloned.1.call-update) | async-done | bytes 131088 | tf_op jit(solution)/shard_map/while/body/eval_jaxpr/psum | solution.py:16
  77.9 1.9 gather_fusion
  79.8 0.2 convert_bitcast_fusion.4
  80.0 0.6 add_convert_fusion.2
  80.7 3.0 %convolution_dynamic-update-slice_fusion.2 = bf16[192,1024]{1,0:T(8,128)(2,1)S(1)} fusion(bf16[192,1024]{1,0:T(8,128)(2,1)S(1)} %get-tuple-element.253, s32[]{:T(128)S(6)} %select_n.154, bf16[2048,1024]{1,0:T(8,128)(2,1)} %get-tuple-element.271, bf16[48,1024]{1,0:T(8,128)(2,1)S(1)} %bitcast.61, bf16[48,1024]{1,0:T(8,128)(2,1)S(1)} %bitcast.62), kind=kOutput, calls=%fused_computation.4.clone.1 | convolution fusion | flops 201719808 | bytes 4587524 | tf_op jit(solution)/shard_map/while/body/eval_jaxpr/dot_general | solution.py:55
  83.8 0.0 all-reduce.3.cloned.1.call-start
  83.8 0.7 broadcast_select_fusion.4
  84.7 3.1 %gather_fusion.1 = bf16[48,2,1024]{2,1,0:T(2,128)(2,1)S(1)} fusion(bf16[2,1024,1024]{2,0,1:T(2,128)(2,1)} %get-tuple-element.268, s32[1024]{0:T(1024)S(1)} %pad_clamp_fusion.5), kind=kCustom, calls=%fused_computation.clone.1 | custom fusion | bytes 393408 | tf_op jit(solution)/shard_map/while/body/eval_jaxpr/jit(_take)/gather | solution.py:46
  87.8 0.2 convert_bitcast_fusion.5
  88.1 33.2 %all-reduce.3.cloned.1.call-done = bf16[2,32,1024]{2,0,1:T(2,128)(2,1)} async-done(((bf16[2,32,1024]{2,0,1:T(2,128)(2,1)}), bf16[2,32,1024]{2,0,1:T(2,128)(2,1)}) %all-reduce.3.cloned.1.call-update) | async-done | bytes 131088 | tf_op jit(solution)/shard_map/while/body/eval_jaxpr/psum | solution.py:16
  121.3 1.9 gather_fusion
  123.1 0.2 convert_bitcast_fusion.4
  123.4 0.6 add_convert_fusion.2
  124.1 3.0 %convolution_dynamic-update-slice_fusion.2 = bf16[192,1024]{1,0:T(8,128)(2,1)S(1)} fusion(bf16[192,1024]{1,0:T(8,128)(2,1)S(1)} %get-tuple-element.253, s32[]{:T(128)S(6)} %select_n.154, bf16[2048,1024]{1,0:T(8,128)(2,1)} %get-tuple-element.271, bf16[48,1024]{1,0:T(8,128)(2,1)S(1)} %bitcast.61, bf16[48,1024]{1,0:T(8,128)(2,1)S(1)} %bitcast.62), kind=kOutput, calls=%fused_computation.4.clone.1 | convolution fusion | flops 201719808 | bytes 4587524 | tf_op jit(solution)/shard_map/while/body/eval_jaxpr/dot_general | solution.py:55
  127.2 0.0 all-reduce.3.cloned.1.call-start
  127.2 0.7 broadcast_select_fusion.4
  128.0 3.1 %gather_fusion.1 = bf16[48,2,1024]{2,1,0:T(2,128)(2,1)S(1)} fusion(bf16[2,1024,1024]{2,0,1:T(2,128)(2,1)} %get-tuple-element.268, s32[1024]{0:T(1024)S(1)} %pad_clamp_fusion.5), kind=kCustom, calls=%fused_computation.clone.1 | custom fusion | bytes 393408 | tf_op jit(solution)/shard_map/while/body/eval_jaxpr/jit(_take)/gather | solution.py:46
  131.2 0.2 convert_bitcast_fusion.5
  131.5 33.2 %all-reduce.3.cloned.1.call-done = bf16[2,32,1024]{2,0,1:T(2,128)(2,1)} async-done(((bf16[2,32,1024]{2,0,1:T(2,128)(2,1)}), bf16[2,32,1024]{2,0,1:T(2,128)(2,1)}) %all-reduce.3.cloned.1.call-update) | async-done | bytes 131088 | tf_op jit(solution)/shard_map/while/body/eval_jaxpr/psum | solution.py:16
  164.7 1.9 gather_fusion
  166.5 0.2 convert_bitcast_fusion.4
  166.8 0.6 add_convert_fusion.2
  167.5 3.0 %convolution_dynamic-update-slice_fusion.2 = bf16[192,1024]{1,0:T(8,128)(2,1)S(1)} fusion(bf16[192,1024]{1,0:T(8,128)(2,1)S(1)} %get-tuple-element.253, s32[]{:T(128)S(6)} %select_n.154, bf16[2048,1024]{1,0:T(8,128)(2,1)} %get-tuple-element.271, bf16[48,1024]{1,0:T(8,128)(2,1)S(1)} %bitcast.61, bf16[48,1024]{1,0:T(8,128)(2,1)S(1)} %bitcast.62), kind=kOutput, calls=%fused_computation.4.clone.1 | convolution fusion | flops 201719808 | bytes 4587524 | tf_op jit(solution)/shard_map/while/body/eval_jaxpr/dot_general | solution.py:55
  170.6 0.7 broadcast_select_fusion.4
  171.4 3.1 %gather_fusion.1 = bf16[48,2,1024]{2,1,0:T(2,128)(2,1)S(1)} fusion(bf16[2,1024,1024]{2,0,1:T(2,128)(2,1)} %get-tuple-element.268, s32[1024]{0:T(1024)S(1)} %pad_clamp_fusion.5), kind=kCustom, calls=%fused_computation.clone.1 | custom fusion | bytes 393408 | tf_op jit(solution)/shard_map/while/body/eval_jaxpr/jit(_take)/gather | solution.py:46
  174.6 0.2 convert_bitcast_fusion.5
  174.8 32.9 %all-reduce.3.cloned.1.call-done = bf16[2,32,1024]{2,0,1:T(2,128)(2,1)} async-done(((bf16[2,32,1024]{2,0,1:T(2,128)(2,1)}), bf16[2,32,1024]{2,0,1:T(2,128)(2,1)}) %all-reduce.3.cloned.1.call-update) | async-done | bytes 131088 | tf_op jit(solution)/shard_map/while/body/eval_jaxpr/psum | solution.py:16
  207.7 1.9 gather_fusion
  209.6 0.2 convert_bitcast_fusion.4
  209.8 0.6 add_convert_fusion.2
  210.5 3.0 %convolution_dynamic-update-slice_fusion.2 = bf16[192,1024]{1,0:T(8,128)(2,1)S(1)} fusion(bf16[192,1024]{1,0:T(8,128)(2,1)S(1)} %get-tuple-element.253, s32[]{:T(128)S(6)} %select_n.154, bf16[2048,1024]{1,0:T(8,128)(2,1)} %get-tuple-element.271, bf16[48,1024]{1,0:T(8,128)(2,1)S(1)} %bitcast.61, bf16[48,1024]{1,0:T(8,128)(2,1)S(1)} %bitcast.62), kind=kOutput, calls=%fused_computation.4.clone.1 | convolution fusion | flops 201719808 | bytes 4587524 | tf_op jit(solution)/shard_map/while/body/eval_jaxpr/dot_general | solution.py:55
  213.6 0.2 reduce-scatter.2.cloned.1.call-start
  213.8 0.5 copy-done
  214.4 0.5 broadcast.190
  214.9 0.7 fusion.17
  215.5 0.1 eq.45
  215.7 1.2 reduce-window.6
  216.9 0.1 slice.56
  216.9 0.1 copy.27
  217.1 0.1 copy.28
  217.2 0.1 add_bitcast_fusion
  217.3 0.1 mul.99
  217.4 0.1 reshape.188
  217.5 1.8 scatter_custom_fusion
  219.3 0.7 all_to_all.12
  219.9 3.4 %all-to-all-start = ((bf16[4,1,96]{2,1,0:T(2,128)(2,1)}), bf16[4,1,96]{2,1,0:T(2,128)(2,1)S(1)}, u32[]{:S(2)}, u32[]{:S(2)}) async-start(bf16[4,1,96]{2,1,0:T(2,128)(2,1)} %all_to_all.12), calls=%async_computation | async-start | bytes 4096 | tf_op jit(solution)/shard_map/all_to_all | solution.py:84
  223.3 13.7 %reduce-scatter.2.cloned.1.call-done = bf16[192,256]{1,0:T(8,128)(2,1)} async-done(((bf16[192,1024]{1,0:T(8,128)(2,1)}), bf16[192,256]{1,0:T(8,128)(2,1)}) %reduce-scatter.2.cloned.1.call-update) | async-done | bytes 98320 | tf_op jit(solution)/shard_map/reduce_scatter | solution.py:64
  237.0 2.2 scatter_custom_fusion.1
  239.3 4.6 %all-to-all-start.1 = ((bf16[4,96,256]{2,1,0:T(8,128)(2,1)}), bf16[4,96,256]{2,1,0:T(8,128)(2,1)S(1)}, u32[]{:S(2)}, u32[]{:S(2)}) async-start(bf16[4,96,256]{2,1,0:T(8,128)(2,1)} %bitcast.16), calls=%async_computation.2 | async-start | bytes 393216 | tf_op jit(solution)/shard_map/all_to_all | solution.py:81
  243.9 0.1 reshape.167
  244.0 7.2 %all-to-all-done.1 = bf16[4,96,256]{2,1,0:T(8,128)(2,1)S(1)} async-done(((bf16[4,96,256]{2,1,0:T(8,128)(2,1)}), bf16[4,96,256]{2,1,0:T(8,128)(2,1)S(1)}, u32[]{:S(2)}, u32[]{:S(2)}) %all-to-all-start.1) | async-done | bytes 196640 | tf_op jit(solution)/shard_map/all_to_all | solution.py:81
  251.2 0.8 fusion.11
  (52 shorter events, 0.8 us)
Async XLA Ops:
  34.8 2.5 copy-start.1
  34.8 2.5 copy-start.2
  37.3 177.5 %copy-start.4 = (s32[1,4,48,1]{2,3,1,0:T(1,128)S(1)}, s32[1,4,48,1]{2,3,1,0:T(1,128)}, u32[]{:S(2)}) copy-start(s32[1,4,48,1]{2,3,1,0:T(1,128)} %param.12) | copy-start | bytes 2308
  37.3 180.0 %copy-start.3 = (s32[1,4,48]{2,1,0:T(4,128)S(1)}, s32[1,4,48]{2,1,0:T(4,128)}, u32[]{:S(2)}) copy-start(s32[1,4,48]{2,1,0:T(4,128)} %param.13) | copy-start | bytes 2308
  37.4 40.5 %all-reduce.3.cloned.1.call-start = ((), (), s32[]{:S(2)}) async-start(), calls=%async_computation.4 | async-start | bytes 262144 | tf_op jit(solution)/shard_map/while/body/eval_jaxpr/psum | solution.py:16
  83.8 37.5 %all-reduce.3.cloned.1.call-start = ((), (), s32[]{:S(2)}) async-start(), calls=%async_computation.4 | async-start | bytes 262144 | tf_op jit(solution)/shard_map/while/body/eval_jaxpr/psum | solution.py:16
  127.2 37.5 %all-reduce.3.cloned.1.call-start = ((), (), s32[]{:S(2)}) async-start(), calls=%async_computation.4 | async-start | bytes 262144 | tf_op jit(solution)/shard_map/while/body/eval_jaxpr/psum | solution.py:16
  170.5 37.2 %all-reduce.3.cloned.1.call-start = ((), (), s32[]{:S(2)}) async-start(), calls=%async_computation.4 | async-start | bytes 262144 | tf_op jit(solution)/shard_map/while/body/eval_jaxpr/psum | solution.py:16
  213.6 0.7 copy-start
  213.6 23.4 %reduce-scatter.2.cloned.1.call-start = ((), (), s32[]{:S(2)}) async-start(), calls=%async_computation.3 | async-start | bytes 491520 | tf_op jit(solution)/shard_map/reduce_scatter | solution.py:64
  219.9 19.4 %all-to-all-start = ((bf16[4,1,96]{2,1,0:T(2,128)(2,1)}), bf16[4,1,96]{2,1,0:T(2,128)(2,1)S(1)}, u32[]{:S(2)}, u32[]{:S(2)}) async-start(bf16[4,1,96]{2,1,0:T(2,128)(2,1)} %all_to_all.12), calls=%async_computation | async-start | bytes 4096 | tf_op jit(solution)/shard_map/all_to_all | solution.py:84
  239.3 11.9 %all-to-all-start.1 = ((bf16[4,96,256]{2,1,0:T(8,128)(2,1)}), bf16[4,96,256]{2,1,0:T(8,128)(2,1)S(1)}, u32[]{:S(2)}, u32[]{:S(2)}) async-start(bf16[4,96,256]{2,1,0:T(8,128)(2,1)} %bitcast.16), calls=%async_computation.2 | async-start | bytes 393216 | tf_op jit(solution)/shard_map/all_to_all | solution.py:81
Sparse Core Ops, SparseCore 0:
  40.5 37.3 all-reduce.2
  86.9 34.3 all-reduce.2
  130.3 34.3 all-reduce.2
  173.3 34.3 all-reduce.2
Sparse Core Ops, SparseCore 1:
  216.6 20.4 reduce-scatter.1
where the time goes:
time: 260 us; the launch traced here: 259 us
  waiting for transfers between devices  156 us (60%)
  local copies, waits for them, and re-layouts  33.3 us (13%)
  other arithmetic  32.9 us (13%)
  between operations  14.7 us (6%)
  matrix products  12.9 us (5%)
  starting transfers between devices  8.39 us (3%)
    psum x4, waiting for transfers between devices, from_root(): return lax.psum(block, axis)  135 us
    another operation x4, other arithmetic  18.8 us
    reduce_scatter x1, waiting for transfers between devices, per_device(): lax.psum_scatter(partial_terms.astype(jnp.bfloat16), ('sub', 'frq'), scat...  13.7 us
    gather x4, local copies, waits for them, and re-layouts, add_pairs(): own_spectra = jnp.take(masked, own_pick, axis=1).astype(jnp.float32)  12.6 us
    dot_general x4, matrix products, add_pairs(): jnp.dot(cross_rows, lag_table, preferred_element_type=jnp.float32)  12.1 us
    gather x4, local copies, waits for them, and re-layouts, add_pairs(): jnp.take(panel_data, partner_pick, axis=1).astype(jnp.float32)  7.43 us
    all_to_all x1, waiting for transfers between devices, per_device(): lax.all_to_all(outgoing.reshape(blocks, CAP, lag_width), 'blk', split_axi...  7.19 us
    while x2, local copies, waits for them, and re-layouts, per_device(): partial_terms = lax.fori_loop(0, blocks, root_turn, empty_terms)  6.44 us
  transfers between devices with their start and end apart: 7, of which 6 were waited for; matrix products, arithmetic and copies ran while one was open for 8% of the time, Pallas kernels for 0%

commit v1 on v0

--- a/solution.py
+++ b/solution.py
@@ -13,7 +13,7 @@
 
 def from_root(block, axis, owner):
     block = jnp.where(lax.axis_index(axis) == owner, block, jnp.zeros_like(block))
-    return lax.psum(block, axis)
+    return jnp.sum(lax.all_gather(block, axis), axis=0)
 
 
 def lag_rows(first_bin, bin_count):

time: 260 us -> 181 us (0.70)
  waiting for transfers between devices: 156 us -> 19 us
  blocking collectives: 0 us -> 64 us
  local copies, waits for them, and re-layouts: 33.3 us -> 30.3 us
    psum x4 -> x0, waiting for transfers between devices: 135 us -> none  [from_root(): return lax.psum(block, axis)]
    all_gather x0 -> x4, blocking collectives: none -> 64 us  [from_root(): return jnp.sum(lax.all_gather(block, axis), axis=0)]
    gather x4, local copies, waits for them, and re-layouts: 7.43 us -> 3.81 us  [add_pairs(): jnp.take(panel_data, partner_pick, axis=1).astype(jnp.float32)]
    select_n x4, other arithmetic: 2.99 us -> 0.06 us  [from_root(): jnp.where(lax.axis_index(axis) == owner, block, jnp.zeros_like(block))]
    while x2 -> x1, local copies, waits for them, and re-layouts: 6.44 us -> 6.24 us  [per_device(): partial_terms = lax.fori_loop(0, blocks, root_turn, empty_terms)]
  transfers between devices with their start and end apart: 7 -> 3, of which waited for: 6 -> 2; matrix products, arithmetic and copies ran while one was open for 8% -> 4% of each run, Pallas kernels for 0% -> 0%
where the time goes in v1:
time: 181 us; the launch traced here: 180 us
  blocking collectives  64 us (35%)
  other arithmetic  30.4 us (17%)
  local copies, waits for them, and re-layouts  30.3 us (17%)
  waiting for transfers between devices  19 us (10%)
  between operations  13.5 us (7%)
  matrix products  12.9 us (7%)
  starting transfers between devices  9.51 us (5%)
    all_gather x4, blocking collectives, from_root(): return jnp.sum(lax.all_gather(block, axis), axis=0)  64 us
    another operation x4, other arithmetic  19 us
    gather x4, local copies, waits for them, and re-layouts, add_pairs(): own_spectra = jnp.take(masked, own_pick, axis=1).astype(jnp.float32)  12.6 us
    dot_general x4, matrix products, add_pairs(): jnp.dot(cross_rows, lag_table, preferred_element_type=jnp.float32)  12.1 us
    reduce_scatter x1, waiting for transfers between devices, per_device(): lax.psum_scatter(partial_terms.astype(jnp.bfloat16), ('sub', 'frq'), scat...  11.8 us
    all_to_all x1, waiting for transfers between devices, per_device(): lax.all_to_all(outgoing.reshape(blocks, CAP, lag_width), 'blk', split_axi...  7.2 us
    while x1, local copies, waits for them, and re-layouts, per_device(): partial_terms = lax.fori_loop(0, blocks, root_turn, empty_terms)  6.24 us
    all_to_all x1, starting transfers between devices, per_device(): lax.all_to_all(labels.reshape(blocks, CAP), 'blk', split_axis=0, concat_a...  4.91 us
  transfers between devices with their start and end apart: 3, of which 2 were waited for; matrix products, arithmetic and copies ran while one was open for 4% of the time, Pallas kernels for 0%

profile of v1, /device:TPU:0, one launch (start us, length us, event | category | flops | bytes accessed | tf_op | source)
XLA Modules:
  0.0 180.1 jit_solution(5382322634119251022)
XLA Ops:
  6.5 0.7 convert_reduce_fusion
  7.2 2.5 %broadcast_multiply_fusion = bf16[2,1024,1024]{2,1,0:T(8,128)(2,1)S(1)} fusion(bf16[2,1024,1024]{2,1,0:T(8,128)(2,1)} %param.8, bf16[1024]{0:T(1024)(128)(2,1)S(1)} %convert_reduce_fusion), kind=kLoop, calls=%fused_computation.41 | loop fusion | flops 2097152 | bytes 8390656 | tf_op jit(solution)/shard_map/mul | solution.py:35
  9.8 6.2 %copy.28 = bf16[2,1024,1024]{2,0,1:T(2,128)(2,1)} copy(bf16[2,1024,1024]{2,1,0:T(8,128)(2,1)S(1)} %broadcast_multiply_fusion) | data formatting | bytes 8388608 | tf_op jit(solution)/shard_map/while | solution.py:63
  16.0 0.2 slice.70
  16.3 17.8 %multiply_convert_fusion.1 = (bf16[1024,1024]{1,0:T(8,128)(2,1)S(1)}, bf16[1024,1024]{1,0:T(8,128)(2,1)S(1)}) fusion(s32[1024]{0:T(1024)S(1)} %get-tuple-element.234, s32[1024]{0:T(1024)S(1)} %get-tuple-element.235), kind=kLoop, calls=%fused_computation.40 | loop fusion | flops 19922944 | bytes 4202496 | tf_op jit(solution)/shard_map/convert.9
  34.0 2.4 %pad_maximum_fusion = bf16[2048,1024]{1,0:T(8,128)(2,1)} fusion(bf16[1024,1024]{1,0:T(8,128)(2,1)S(1)} %get-tuple-element.233, bf16[1024,1024]{1,0:T(8,128)(2,1)S(1)} %get-tuple-element.232), kind=kLoop, calls=%fused_computation.38 | loop fusion | flops 8388608 | bytes 8388608 | tf_op jit(solution)/shard_map/concatenate | solution.py:26
  36.6 98.8 %while.15 = (s32[]{:T(128)}, bf16[192,1024]{1,0:T(8,128)(2,1)S(1)}, s32[4,48]{1,0:T(4,128)S(1)}, bf16[2,1024,1024]{2,0,1:T(2,128)(2,1)}, s32[4,48]{1,0:T(4,128)S...) while((s32[]{:T(128)}, bf16[192,1024]{1,0:T(8,128)(2,1)S(1)}, ...), condition=%wide.region_6.7_spmd, body=%wide.region_4.6_spmd.sunk | while | flops 202771312 | bytes 9775403 | solution.py:63
  36.6 17.4 %all-gather.2 = bf16[8,32,1024]{2,1,0:T(8,128)(2,1)S(1)} all-gather(bf16[2,32,1024]{2,1,0:T(8,128)(2,1)S(1)} %broadcast_select_fusion.4), channel_id=2, replica_groups=mesh['grp'=2,'blk'=4,'sub'=2,'frq'=2] {'blk'}, dimensions={0}, use_global_device_ids=true | all-gather | bytes 655360 | tf_op jit(solution)/shard_map/while/body/eval_jaxpr/all_gather | solution.py:16
  54.0 0.1 reduce_sum.29
  54.1 0.1 copy.44
  54.2 1.0 gather_fusion
  55.2 0.2 convert_bitcast_fusion.4
  55.5 3.1 %gather_fusion.1 = bf16[48,2,1024]{2,1,0:T(2,128)(2,1)S(1)} fusion(bf16[2,1024,1024]{2,0,1:T(2,128)(2,1)} %get-tuple-element.322, s32[1024]{0:T(1024)S(1)} %pad_clamp_fusion.5), kind=kCustom, calls=%fused_computation.clone.1 | custom fusion | bytes 393408 | tf_op jit(solution)/shard_map/while/body/eval_jaxpr/jit(_take)/gather | solution.py:46
  58.6 0.2 convert_bitcast_fusion.5
  58.9 0.6 add_convert_fusion.2
  59.6 3.0 %convolution_dynamic-update-slice_fusion.2 = bf16[192,1024]{1,0:T(8,128)(2,1)S(1)} fusion(bf16[192,1024]{1,0:T(8,128)(2,1)S(1)} %get-tuple-element.306, s32[]{:T(128)S(6)} %select_n.189, bf16[2048,1024]{1,0:T(8,128)(2,1)} %get-tuple-element.325, bf16[48,1024]{1,0:T(8,128)(2,1)S(1)} %bitcast.65, bf16[48,1024]{1,0:T(8,128)(2,1)S(1)} %bitcast.66), kind=kOutput, calls=%fused_computation.4.clone.1 | convolution fusion | flops 201719808 | bytes 4587524 | tf_op jit(solution)/shard_map/while/body/eval_jaxpr/dot_general | solution.py:55
  62.7 16.3 %all-gather.2 = bf16[8,32,1024]{2,1,0:T(8,128)(2,1)S(1)} all-gather(bf16[2,32,1024]{2,1,0:T(8,128)(2,1)S(1)} %broadcast_select_fusion.4), channel_id=2, replica_groups=mesh['grp'=2,'blk'=4,'sub'=2,'frq'=2] {'blk'}, dimensions={0}, use_global_device_ids=true | all-gather | bytes 655360 | tf_op jit(solution)/shard_map/while/body/eval_jaxpr/all_gather | solution.py:16
  79.0 0.1 reduce_sum.29
  79.0 0.1 copy.44
  79.2 1.0 gather_fusion
  80.2 0.2 convert_bitcast_fusion.4
  80.4 3.1 %gather_fusion.1 = bf16[48,2,1024]{2,1,0:T(2,128)(2,1)S(1)} fusion(bf16[2,1024,1024]{2,0,1:T(2,128)(2,1)} %get-tuple-element.322, s32[1024]{0:T(1024)S(1)} %pad_clamp_fusion.5), kind=kCustom, calls=%fused_computation.clone.1 | custom fusion | bytes 393408 | tf_op jit(solution)/shard_map/while/body/eval_jaxpr/jit(_take)/gather | solution.py:46
  83.6 0.2 convert_bitcast_fusion.5
  83.8 0.6 add_convert_fusion.2
  84.5 3.0 %convolution_dynamic-update-slice_fusion.2 = bf16[192,1024]{1,0:T(8,128)(2,1)S(1)} fusion(bf16[192,1024]{1,0:T(8,128)(2,1)S(1)} %get-tuple-element.306, s32[]{:T(128)S(6)} %select_n.189, bf16[2048,1024]{1,0:T(8,128)(2,1)} %get-tuple-element.325, bf16[48,1024]{1,0:T(8,128)(2,1)S(1)} %bitcast.65, bf16[48,1024]{1,0:T(8,128)(2,1)S(1)} %bitcast.66), kind=kOutput, calls=%fused_computation.4.clone.1 | convolution fusion | flops 201719808 | bytes 4587524 | tf_op jit(solution)/shard_map/while/body/eval_jaxpr/dot_general | solution.py:55
  87.7 15.6 %all-gather.2 = bf16[8,32,1024]{2,1,0:T(8,128)(2,1)S(1)} all-gather(bf16[2,32,1024]{2,1,0:T(8,128)(2,1)S(1)} %broadcast_select_fusion.4), channel_id=2, replica_groups=mesh['grp'=2,'blk'=4,'sub'=2,'frq'=2] {'blk'}, dimensions={0}, use_global_device_ids=true | all-gather | bytes 655360 | tf_op jit(solution)/shard_map/while/body/eval_jaxpr/all_gather | solution.py:16
  103.2 0.1 reduce_sum.29
  103.3 0.1 copy.44
  103.5 1.0 gather_fusion
  104.4 0.2 convert_bitcast_fusion.4
  104.7 3.1 %gather_fusion.1 = bf16[48,2,1024]{2,1,0:T(2,128)(2,1)S(1)} fusion(bf16[2,1024,1024]{2,0,1:T(2,128)(2,1)} %get-tuple-element.322, s32[1024]{0:T(1024)S(1)} %pad_clamp_fusion.5), kind=kCustom, calls=%fused_computation.clone.1 | custom fusion | bytes 393408 | tf_op jit(solution)/shard_map/while/body/eval_jaxpr/jit(_take)/gather | solution.py:46
  107.9 0.2 convert_bitcast_fusion.5
  108.1 0.6 add_convert_fusion.2
  108.8 3.0 %convolution_dynamic-update-slice_fusion.2 = bf16[192,1024]{1,0:T(8,128)(2,1)S(1)} fusion(bf16[192,1024]{1,0:T(8,128)(2,1)S(1)} %get-tuple-element.306, s32[]{:T(128)S(6)} %select_n.189, bf16[2048,1024]{1,0:T(8,128)(2,1)} %get-tuple-element.325, bf16[48,1024]{1,0:T(8,128)(2,1)S(1)} %bitcast.65, bf16[48,1024]{1,0:T(8,128)(2,1)S(1)} %bitcast.66), kind=kOutput, calls=%fused_computation.4.clone.1 | convolution fusion | flops 201719808 | bytes 4587524 | tf_op jit(solution)/shard_map/while/body/eval_jaxpr/dot_general | solution.py:55
  111.9 14.8 %all-gather.2 = bf16[8,32,1024]{2,1,0:T(8,128)(2,1)S(1)} all-gather(bf16[2,32,1024]{2,1,0:T(8,128)(2,1)S(1)} %broadcast_select_fusion.4), channel_id=2, replica_groups=mesh['grp'=2,'blk'=4,'sub'=2,'frq'=2] {'blk'}, dimensions={0}, use_global_device_ids=true | all-gather | bytes 655360 | tf_op jit(solution)/shard_map/while/body/eval_jaxpr/all_gather | solution.py:16
  126.7 0.1 reduce_sum.29
  126.8 0.1 copy.44
  126.9 1.0 gather_fusion
  127.9 0.2 convert_bitcast_fusion.4
  128.2 3.1 %gather_fusion.1 = bf16[48,2,1024]{2,1,0:T(2,128)(2,1)S(1)} fusion(bf16[2,1024,1024]{2,0,1:T(2,128)(2,1)} %get-tuple-element.322, s32[1024]{0:T(1024)S(1)} %pad_clamp_fusion.5), kind=kCustom, calls=%fused_computation.clone.1 | custom fusion | bytes 393408 | tf_op jit(solution)/shard_map/while/body/eval_jaxpr/jit(_take)/gather | solution.py:46
  131.3 0.2 convert_bitcast_fusion.5
  131.6 0.6 add_convert_fusion.2
  132.3 3.0 %convolution_dynamic-update-slice_fusion.2 = bf16[192,1024]{1,0:T(8,128)(2,1)S(1)} fusion(bf16[192,1024]{1,0:T(8,128)(2,1)S(1)} %get-tuple-element.306, s32[]{:T(128)S(6)} %select_n.189, bf16[2048,1024]{1,0:T(8,128)(2,1)} %get-tuple-element.325, bf16[48,1024]{1,0:T(8,128)(2,1)S(1)} %bitcast.65, bf16[48,1024]{1,0:T(8,128)(2,1)S(1)} %bitcast.66), kind=kOutput, calls=%fused_computation.4.clone.1 | convolution fusion | flops 201719808 | bytes 4587524 | tf_op jit(solution)/shard_map/while/body/eval_jaxpr/dot_general | solution.py:55
  135.4 0.7 copy-done
  136.1 0.0 reduce-scatter.2.cloned.1.call-update
  136.1 0.5 broadcast.246
  136.6 0.7 fusion.17
  137.3 0.1 eq.48
  137.4 1.2 reduce-window.6
  138.6 0.1 slice.68
  138.7 0.1 copy.25
  138.8 0.1 copy.26
  138.9 0.1 add_bitcast_fusion
  139.0 0.1 mul.114
  139.1 0.1 reshape.223
  139.2 1.8 scatter_custom_fusion
  141.0 0.7 all_to_all.12
  141.7 4.9 %all-to-all-start = ((bf16[4,1,96]{2,1,0:T(2,128)(2,1)}), bf16[4,1,96]{2,1,0:T(2,128)(2,1)S(1)}, u32[]{:S(2)}, u32[]{:S(2)}) async-start(bf16[4,1,96]{2,1,0:T(2,128)(2,1)} %all_to_all.12), calls=%async_computation | async-start | bytes 4096 | tf_op jit(solution)/shard_map/all_to_all | solution.py:84
  146.6 11.8 %reduce-scatter.2.cloned.1.call-done = bf16[192,256]{1,0:T(8,128)(2,1)} async-done(((bf16[192,1024]{1,0:T(8,128)(2,1)}), bf16[192,256]{1,0:T(8,128)(2,1)}) %reduce-scatter.2.cloned.1.call-update) | async-done | bytes 98320 | tf_op jit(solution)/shard_map/reduce_scatter | solution.py:64
  158.3 2.2 %scatter_custom_fusion.1 = bf16[384,256]{1,0:T(8,128)(2,1)} fusion(s32[192]{0:T(256)S(1)} %bitcast.75, bf16[192,256]{1,0:T(8,128)(2,1)} %reduce-scatter.2.cloned.1.call-done, bf16[]{:T(256)} %constant.195.clone.1), kind=kCustom, calls=%fused_computation.43 | custom fusion | bytes 197120 | tf_op jit(solution)/shard_map/scatter | solution.py:74
  160.6 4.6 %all-to-all-start.1 = ((bf16[4,96,256]{2,1,0:T(8,128)(2,1)}), bf16[4,96,256]{2,1,0:T(8,128)(2,1)S(1)}, u32[]{:S(2)}, u32[]{:S(2)}) async-start(bf16[4,96,256]{2,1,0:T(8,128)(2,1)} %bitcast.16), calls=%async_computation.2 | async-start | bytes 393216 | tf_op jit(solution)/shard_map/all_to_all | solution.py:81
  165.2 0.1 reshape.202
  165.3 7.2 %all-to-all-done.1 = bf16[4,96,256]{2,1,0:T(8,128)(2,1)S(1)} async-done(((bf16[4,96,256]{2,1,0:T(8,128)(2,1)}), bf16[4,96,256]{2,1,0:T(8,128)(2,1)S(1)}, u32[]{:S(2)}, u32[]{:S(2)}) %all-to-all-start.1) | async-done | bytes 196640 | tf_op jit(solution)/shard_map/all_to_all | solution.py:81
  172.5 0.8 fusion.11
  (52 shorter events, 0.8 us)
Async XLA Ops:
  6.5 151.8 %reduce-scatter.2.cloned.1.call-start = ((), (), s32[]{:S(2)}) async-start(), calls=%async_computation.3 | async-start | bytes 491520 | tf_op jit(solution)/shard_map/reduce_scatter | solution.py:64
  34.0 2.5 %copy-start.1 = (s32[1,4,48]{2,1,0:T(4,128)S(1)}, s32[1,4,48]{2,1,0:T(4,128)}, u32[]{:S(2)}) copy-start(s32[1,4,48]{2,1,0:T(4,128)} %param.10) | copy-start | bytes 2308
  34.0 2.5 %copy-start.2 = (s32[1,4,48]{2,1,0:T(4,128)S(1)}, s32[1,4,48]{2,1,0:T(4,128)}, u32[]{:S(2)}) copy-start(s32[1,4,48]{2,1,0:T(4,128)} %param.11) | copy-start | bytes 2308
  36.5 100.1 %copy-start.4 = (s32[1,4,48,1]{2,3,1,0:T(1,128)S(1)}, s32[1,4,48,1]{2,3,1,0:T(1,128)}, u32[]{:S(2)}) copy-start(s32[1,4,48,1]{2,3,1,0:T(1,128)} %param.12) | copy-start | bytes 2308
  36.5 102.6 %copy-start.3 = (s32[1,4,48]{2,1,0:T(4,128)S(1)}, s32[1,4,48]{2,1,0:T(4,128)}, u32[]{:S(2)}) copy-start(s32[1,4,48]{2,1,0:T(4,128)} %param.13) | copy-start | bytes 2308
  135.3 0.7 copy-start
  141.7 18.9 %all-to-all-start = ((bf16[4,1,96]{2,1,0:T(2,128)(2,1)}), bf16[4,1,96]{2,1,0:T(2,128)(2,1)S(1)}, u32[]{:S(2)}, u32[]{:S(2)}) async-start(bf16[4,1,96]{2,1,0:T(2,128)(2,1)} %all_to_all.12), calls=%async_computation | async-start | bytes 4096 | tf_op jit(solution)/shard_map/all_to_all | solution.py:84
  160.6 11.9 %all-to-all-start.1 = ((bf16[4,96,256]{2,1,0:T(8,128)(2,1)}), bf16[4,96,256]{2,1,0:T(8,128)(2,1)S(1)}, u32[]{:S(2)}, u32[]{:S(2)}) async-start(bf16[4,96,256]{2,1,0:T(8,128)(2,1)} %bitcast.16), calls=%async_computation.2 | async-start | bytes 393216 | tf_op jit(solution)/shard_map/all_to_all | solution.py:81
Sparse Core Ops, SparseCore 0:
  136.2 22.0 reduce-scatter.1
